TPU v7x, 32 devices: a whole 2x2x4 slice. The times are simulated.
32 devices in a mesh: dp: 2 (over core), ctx: 4 (over z), tp: 4 (over y, x).
Axes of the slice: x: 2, y: 2, z: 4, core: 2. Of those that a mesh axis runs over, the one named last changes fastest.
Arguments:
- projected: bfloat16 [2, 3, 512, 4096], P('dp', None, 'ctx', 'tp'), may hold values from -6 to 6
- cotangent: bfloat16 [2, 512, 4096], P('dp', 'ctx', 'tp'), may hold values from -6 to 6
- conv_taps: float32 [3, 7, 4096], P(None, None, 'tp'), may hold values from -2 to 2
- residues: float32 [16, 4096], P(None, 'tp'), may hold values from -1.5 to 1.5
- decay_rates: float32 [16, 4096], P(None, 'tp'), may hold values from 0.00048828125 to 0.0625, as said below
- skip_gain: float32 [4096], P('tp'), may hold values from 0.1 to 1.9
Outputs:
- mixed: bfloat16 [2, 512, 4096], P('dp', 'ctx', 'tp')
- input_grad: bfloat16 [2, 3, 512, 4096], P('dp', None, 'ctx', 'tp')
- taps_update: float32 [3, 7, 4096], P(None, None, 'tp')
- residue_update: float32 [16, 4096], P(None, 'tp')
- rate_update: float32 [16, 4096], P(None, 'tp')
- skip_update: float32 [4096], P('tp')
Inputs may be any that keep to these rules, and one draw needn't show every extreme that they name: `decay_rates`: decay rates of the poles; positive.
All inputs are finite; a program needn't handle non-finite values.
Results may differ from a plain program's by a relative error of at most 0.0013.
Values may be sent and summed in bfloat16 or wider, within the bound.
A program may use at most 64 MiB of HBM per device.

v0:
```python
import functools
import jax
import jax.numpy as jnp
from jax import lax
from jax.experimental import pallas as pl
from jax.experimental.pallas import tpu as pltpu
from jax.sharding import PartitionSpec as P


def prefix(x, axis, combine, identity, reverse):
    peers, mine = (lax.axis_size(axis), lax.axis_index(axis))
    everything = jax.tree.map(lambda part: lax.all_gather(part, axis), x)
    start = jax.tree.map(
        lambda part, zero: jnp.broadcast_to(jnp.asarray(zero, part.dtype), part.shape), x, identity
    )

    def step(k, before):
        at = peers - 1 - k if reverse else k
        reached = at > mine if reverse else at < mine
        new = combine(before, jax.tree.map(lambda part: part[at], everything))
        return jax.tree.map(lambda a, b: jnp.where(reached, a, b), new, before)

    return lax.fori_loop(0, peers, step, start)


def shifted(block, axis, distance):
    devices = range(lax.axis_size(axis))
    route = [(i - distance, i) for i in devices if i - distance in devices]
    return lax.ppermute(block, axis, route)


def linear_combine(earlier, later):
    return (earlier[0] * later[0], later[0] * earlier[1] + later[1])


def carry_pass(block_decay, summary, backward):
    identity = (jnp.ones_like(summary), jnp.zeros_like(summary))
    return prefix((block_decay, summary), "ctx", linear_combine, identity, backward)[1]


def local(projected, cotangent, conv_taps, residues, decay_rates, skip_gain):
    streams = projected[0]
    tok_rows = streams.shape[1]
    width = streams.shape[2]
    order = residues.shape[0]
    tap_count = conv_taps.shape[1]
    edge_rows = tap_count - 1
    prev_rows = shifted(streams[:, tok_rows - edge_rows :, :], "ctx", 1)
    padded = jnp.concatenate([prev_rows, streams], axis=1).astype(jnp.float32)
    features = conv_taps[:, 0, None, :] * padded[:, edge_rows : edge_rows + tok_rows, :]
    for offset in range(1, tap_count):
        features = (
            features
            + conv_taps[:, offset, None, :]
            * padded[:, edge_rows - offset : edge_rows - offset + tok_rows, :]
        )
    query = features[0]
    keyed = features[1]
    valued = features[2]
    drive = keyed * valued
    decays = jnp.exp(-decay_rates)
    root_norm = jnp.sqrt(-jnp.expm1(-2.0 * decay_rates))
    coeffs = residues * root_norm
    cot_rows = cotangent[0].astype(jnp.float32)
    grad_z = cot_rows * query
    zeros_state = jnp.zeros((order, width), jnp.float32)

    def local_step(carried, rows):
        state_now, adj_now = carried
        drive_row, grad_row = rows
        state_now = decays * state_now + drive_row[None, :]
        adj_now = decays * adj_now + coeffs * grad_row[None, :]
        return ((state_now, adj_now), None)

    (end_state, first_adjoint), _ = lax.scan(
        local_step, (zeros_state, zeros_state), (drive, grad_z[::-1]), unroll=8
    )
    block_decay = jnp.exp(-decay_rates * tok_rows)
    state_in = carry_pass(block_decay, end_state, False)
    adjoint_in = carry_pass(block_decay, first_adjoint, True)

    def forward_step(carried, rows):
        state_now, coeff_acc = carried
        drive_row, grad_row = rows
        before = state_now
        state_now = decays * state_now + drive_row[None, :]
        coeff_acc = coeff_acc + grad_row[None, :] * state_now
        return ((state_now, coeff_acc), (before, jnp.sum(coeffs * state_now, axis=0)))

    (_, coeff_grad), (state_prev, long_term) = lax.scan(
        forward_step, (state_in, zeros_state), (drive, grad_z), unroll=8
    )

    def backward_step(carried, rows):
        adj_now, decay_acc = carried
        grad_row, before = rows
        adj_now = decays * adj_now + coeffs * grad_row[None, :]
        decay_acc = decay_acc + adj_now * before
        return ((adj_now, decay_acc), jnp.sum(adj_now, axis=0))

    (_, decay_grad), adjoint_total = lax.scan(
        backward_step, (adjoint_in, zeros_state), (grad_z, state_prev), reverse=True, unroll=8
    )
    mixer_out = long_term + skip_gain * drive
    mixed = (query * mixer_out).astype(jnp.bfloat16)[None]
    grad_drive = adjoint_total + skip_gain * grad_z
    feature_grad = jnp.stack(
        [cot_rows * mixer_out, grad_drive * valued, grad_drive * keyed], axis=0
    )
    next_rows = shifted(feature_grad[:, :edge_rows, :], "ctx", -1)
    grad_padded = jnp.concatenate([feature_grad, next_rows], axis=1)
    stream_grad = conv_taps[:, 0, None, :] * grad_padded[:, 0:tok_rows, :]
    for offset in range(1, tap_count):
        stream_grad = (
            stream_grad
            + conv_taps[:, offset, None, :] * grad_padded[:, offset : offset + tok_rows, :]
        )
    input_grad = stream_grad.astype(jnp.bfloat16)[None]
    taps_grad = jnp.stack(
        [
            jnp.sum(
                feature_grad * padded[:, edge_rows - offset : edge_rows - offset + tok_rows, :],
                axis=1,
            )
            for offset in range(tap_count)
        ],
        axis=1,
    )
    skip_grad = jnp.sum(grad_z * drive, axis=0)
    residue_grad = coeff_grad * root_norm
    rate_grad = -decays * decay_grad + coeff_grad * residues * decays * decays / root_norm
    grad_sums = lax.psum((taps_grad, residue_grad, rate_grad, skip_grad), ("dp", "ctx"))
    totals = lax.psum(tuple((jnp.sum(member * member) for member in grad_sums)), "tp")
    full_width = width * lax.axis_size("tp")
    entries = (3 * tap_count * full_width, order * full_width, order * full_width, full_width)
    updates = [
        member / jnp.maximum(1.0, jnp.sqrt(total / entry_count))
        for member, total, entry_count in zip(grad_sums, totals, entries)
    ]
    return (mixed, input_grad, updates[0], updates[1], updates[2], updates[3])


LANES = 128
SUBL = 8
HALO = 8
GROUP = 4
MESH = pl.DeviceIdType.MESH
F32 = jnp.float32


def iota_rows():
    return lax.broadcasted_iota(jnp.int32, (SUBL, LANES), 0)


def mega(sizes, x, cot, taps, res, rate, skip, norm, mixed, ig, upd,
         prev, nxt, nct, xs, ct, feat, drive, gz, pre_f, pre_b, sum_f, sum_b, got_f, got_b,
         tab, in_f, in_b, lt, at, hist, acc_c, acc_d, ms, fg, grads, rs, ag, tot, tot_tp, tot_all,
         halo_send, halo_recv, f_send, f_recv, b_send, b_recv,
         rs_send, rs_recv, ag_send, ag_recv, tp_send, tp_recv, all_send, all_recv):
    ndp, nctx, ntp, order, tap_count = sizes
    tok, width = cot.shape
    blocks = width // LANES
    group = ndp * nctx
    seg = (tok + HALO) // SUBL
    last = seg - 1 - HALO
    grad_rows = grads.shape[1]
    me_dp = lax.axis_index("dp")
    me = lax.axis_index("ctx")
    me_tp = lax.axis_index("tp")
    me_g = me_dp * nctx + me

    def peer(p):
        return {"dp": p // nctx, "ctx": lax.rem(p, nctx)}

    barrier = pltpu.get_barrier_semaphore()
    for k in range(1, group):
        p = lax.rem(me_g + k, group)
        pl.semaphore_signal(barrier, inc=1, device_id=peer(p), device_id_type=MESH)
    for k in range(1, ntp):
        q = lax.rem(me_tp + k, ntp)
        pl.semaphore_signal(barrier, inc=1, device_id={"tp": q}, device_id_type=MESH)
    pl.semaphore_wait(barrier, group - 1 + ntp - 1)

    def remote(src, dst, send, recv, where):
        return pltpu.make_async_remote_copy(
            src_ref=src, dst_ref=dst, send_sem=send, recv_sem=recv,
            device_id=where, device_id_type=MESH)

    down = remote(x.at[:, pl.ds(tok - HALO, HALO), :], prev, halo_send.at[0], halo_recv.at[0],
                  {"ctx": jnp.minimum(me + 1, nctx - 1)})
    up = remote(x.at[:, pl.ds(0, HALO), :], nxt, halo_send.at[1], halo_recv.at[1],
                {"ctx": jnp.maximum(me - 1, 0)})
    upc = remote(cot.at[pl.ds(0, HALO), :], nct, halo_send.at[2], halo_recv.at[2],
                 {"ctx": jnp.maximum(me - 1, 0)})

    @pl.when(me < nctx - 1)
    def _():
        down.start()

    @pl.when(me > 0)
    def _():
        up.start()
        upc.start()

    @pl.when(me == 0)
    def _():
        prev[...] = jnp.zeros_like(prev)

    @pl.when(me == nctx - 1)
    def _():
        nxt[...] = jnp.zeros_like(nxt)
        nct[...] = jnp.zeros_like(nct)

    @pl.when(me > 0)
    def _():
        down.wait_recv()

    @pl.when(me < nctx - 1)
    def _():
        up.wait_recv()
        upc.wait_recv()

    def lanes(b):
        return pl.ds(pl.multiple_of(b * LANES, LANES), LANES)

    def row(ref, n, b):
        return jnp.broadcast_to(ref[pl.ds(n, 1), lanes(b)], (SUBL, LANES))

    def trow(k, b, n):
        return jnp.broadcast_to(tab[k, b, pl.ds(n, 1), :], (SUBL, LANES))

    def at_j(j):
        return pl.ds(j * SUBL, SUBL)

    def strided(j):
        return pl.ds(j, SUBL, stride=seg)

    def f_copy(b, far):
        return remote(sum_f.at[b], got_f.at[far - 1, b], f_send.at[far - 1, b], f_recv.at[far - 1, b],
                      {"ctx": jnp.minimum(me + far, nctx - 1)})

    def b_copy(b, far):
        return remote(sum_b.at[b], got_b.at[far - 1, b], b_send.at[far - 1, b], b_recv.at[far - 1, b],
                      {"ctx": jnp.maximum(me - far, 0)})

    def first(i, carry):
        b = lax.rem(me_g + 1 + i, blocks)
        lo = lanes(b)
        rates = rate[:, lo]
        tab[0, b] = jnp.exp(-rates)
        tab[1, b] = jnp.exp(-rates * seg)
        tab[2, b] = jnp.exp(-rates * (2 * seg))
        tab[3, b] = jnp.exp(-rates * (4 * seg))
        tab[4, b] = jnp.exp(-rates * (seg - HALO))
        root = norm[:, lo]
        tab[5, b] = root
        tab[6, b] = res[:, lo] * root
        tab[7, b] = rates
        for s in range(3):
            xs[b, s, 0:HALO, :] = prev[s, :, lo].astype(F32)
            xs[b, s, tok + HALO : tok + 2 * HALO, :] = nxt[s, :, lo].astype(F32)
            for r in range(tok // 16):
                xs[b, s, HALO + 16 * r : HALO + 16 * r + 16, :] = x[s, 16 * r : 16 * r + 16, lo].astype(F32)
        ct[b, tok : tok + HALO, :] = nct[:, lo].astype(F32)
        for r in range(tok // 16):
            ct[b, 16 * r : 16 * r + 16, :] = cot[16 * r : 16 * r + 16, lo].astype(F32)
        for s in range(3):
            w = [row(taps, s * tap_count + o, b) for o in range(tap_count)]
            for j in range(seg):
                total = w[0] * xs[b, s, strided(HALO + j), :]
                for o in range(1, tap_count):
                    total = total + w[o] * xs[b, s, strided(HALO + j - o), :]
                feat[b, s, at_j(j), :] = total
                if s == 0:
                    gz[b, at_j(j), :] = total * ct[b, strided(j), :]
                if s == 2:
                    drive[b, at_j(j), :] = total * feat[b, 1, at_j(j), :]
        rows_at = iota_rows()

        def modes(g, c):
            ns = [g * GROUP + m for m in range(GROUP)]
            d = [trow(0, b, n) for n in ns]
            s = [drive[b, at_j(0), :]] * GROUP
            a = [gz[b, at_j(seg - 1), :]] * GROUP
            mid_s = s if last == 0 else None
            mid_a = a if seg - 1 == HALO else None
            for j in range(1, seg):
                dr = drive[b, at_j(j), :]
                gr = gz[b, at_j(seg - 1 - j), :]
                s = [d[m] * s[m] + dr for m in range(GROUP)]
                a = [d[m] * a[m] + gr for m in range(GROUP)]
                if j == last:
                    mid_s = s
                if seg - 1 - j == HALO:
                    mid_a = a
            for m, n in enumerate(ns):
                y, z = s[m], a[m]
                for k, far in ((1, 1), (2, 2), (3, 4)):
                    p = trow(k, b, n)
                    y = y + jnp.where(rows_at >= far, p * pltpu.roll(y, far, 0), 0.0)
                    z = z + jnp.where(rows_at < SUBL - far, p * pltpu.roll(z, SUBL - far, 0), 0.0)
                y = jnp.where(rows_at >= 1, pltpu.roll(y, 1, 0), 0.0)
                z = jnp.where(rows_at < SUBL - 1, pltpu.roll(z, SUBL - 1, 0), 0.0)
                pre_f[b, n] = y
                pre_b[b, n] = z
                p = trow(4, b, n)
                sum_f[b, pl.ds(n, 1), :] = (mid_s[m] + p * y)[SUBL - 1 : SUBL, :]
                sum_b[b, pl.ds(n, 1), :] = (mid_a[m] + p * z)[0:1, :]
            return c

        lax.fori_loop(0, order // GROUP, modes, 0)
        for far in range(1, nctx):
            @pl.when(me + far < nctx)
            def _():
                f_copy(b, far).start()

            @pl.when(me >= far)
            def _():
                b_copy(b, far).start()
        return carry

    lax.fori_loop(0, blocks, first, 0)

    def rs_copy(b):
        return remote(grads.at[b], rs.at[me_g], rs_send.at[b], rs_recv.at[me_g], peer(b))

    def second(i, carry):
        b = lax.rem(me_g + 1 + i, blocks)
        lo = lanes(b)
        rates = rate[:, lo]
        in_f[...] = jnp.zeros_like(in_f)
        in_b[...] = jnp.zeros_like(in_b)
        for far in range(1, nctx):
            scale = jnp.exp(-rates * (tok * (far - 1)))

            @pl.when(me >= far)
            def _():
                f_copy(b, far).wait_recv()
                in_f[...] += scale * got_f[far - 1, b]

            @pl.when(me + far < nctx)
            def _():
                b_copy(b, far).wait_recv()
                in_b[...] += scale * got_b[far - 1, b]
        lt[...] = jnp.zeros_like(lt)
        at[...] = jnp.zeros_like(at)
        rows_at = iota_rows()
        seg_f = rows_at.astype(F32) * (-float(seg))
        seg_b = (SUBL - 1 - rows_at).astype(F32) * (-float(seg))
        zero = jnp.zeros((SUBL, LANES), F32)

        def fold(head, rest):
            return jnp.sum(head + jnp.where(rows_at < SUBL - 1, rest, 0.0), axis=0, keepdims=True)

        def modes(g, carried):
            ns = [g * GROUP + m for m in range(GROUP)]
            d = [trow(0, b, n) for n in ns]
            c = [trow(6, b, n) for n in ns]
            rr = [trow(7, b, n) for n in ns]
            s = [pre_f[b, n] + jnp.exp(seg_f * rr[m]) * jnp.broadcast_to(in_f[pl.ds(n, 1), :], (SUBL, LANES))
                 for m, n in enumerate(ns)]
            a = [pre_b[b, n] + jnp.exp(seg_b * rr[m]) * jnp.broadcast_to(in_b[pl.ds(n, 1), :], (SUBL, LANES))
                 for m, n in enumerate(ns)]
            head, rest = [zero] * GROUP, [zero] * GROUP
            for j in range(seg):
                dr = drive[b, at_j(j), :]
                gr = gz[b, at_j(j), :]
                for m in range(GROUP):
                    hist[m, j] = s[m]
                s = [d[m] * s[m] + dr for m in range(GROUP)]
                out = lt[at_j(j), :]
                for m in range(GROUP):
                    out = out + c[m] * s[m]
                lt[at_j(j), :] = out
                if j <= last:
                    head = [head[m] + gr * s[m] for m in range(GROUP)]
                else:
                    rest = [rest[m] + gr * s[m] for m in range(GROUP)]
            for m, n in enumerate(ns):
                acc_c[pl.ds(n, 1), :] = fold(head[m], rest[m])
            head, rest = [zero] * GROUP, [zero] * GROUP
            for j in reversed(range(seg)):
                gr = gz[b, at_j(j), :]
                a = [d[m] * a[m] + gr for m in range(GROUP)]
                out = at[at_j(j), :]
                for m in range(GROUP):
                    out = out + c[m] * a[m]
                at[at_j(j), :] = out
                if j <= last:
                    head = [head[m] + a[m] * hist[m, j] for m in range(GROUP)]
                else:
                    rest = [rest[m] + a[m] * hist[m, j] for m in range(GROUP)]
            for m, n in enumerate(ns):
                acc_d[pl.ds(n, 1), :] = fold(head[m], rest[m])
            return carried

        lax.fori_loop(0, order // GROUP, modes, 0)
        decays, root, coeffs = tab[0, b], tab[5, b], tab[6, b]
        coeff_grad = acc_c[...]
        grads[b, 0:order, :] = coeff_grad * root
        grads[b, order : 2 * order, :] = (
            -decays * (coeffs * acc_d[...]) + coeff_grad * res[:, lo] * decays * decays / root)
        gain = row(skip, 0, b)
        head, rest = zero, zero
        for j in range(seg):
            dr = drive[b, at_j(j), :]
            gr = gz[b, at_j(j), :]
            mixer = lt[at_j(j), :] + gain * dr
            ms[strided(j), :] = feat[b, 0, at_j(j), :] * mixer
            fg[0, strided(j), :] = ct[b, strided(j), :] * mixer
            grad_drive = at[at_j(j), :] + gain * gr
            fg[1, strided(j), :] = grad_drive * feat[b, 2, at_j(j), :]
            fg[2, strided(j), :] = grad_drive * feat[b, 1, at_j(j), :]
            if j <= last:
                head = head + gr * dr
            else:
                rest = rest + gr * dr
        base = 2 * order
        grads[b, base + 3 * tap_count : base + 3 * tap_count + 1, :] = fold(head, rest)
        pad = grad_rows - (base + 3 * tap_count + 1)
        grads[b, base + 3 * tap_count + 1 : grad_rows, :] = jnp.zeros((pad, LANES), F32)
        for r in range(tok // 16):
            mixed[16 * r : 16 * r + 16, lo] = ms[16 * r : 16 * r + 16, :].astype(mixed.dtype)
        for s in range(3):
            w = [row(taps, s * tap_count + o, b) for o in range(tap_count)]
            sums = [zero] * tap_count
            for r in range(tok // 16):
                parts = []
                for half in range(2):
                    at_row = 16 * r + 8 * half
                    here = fg[s, at_row : at_row + SUBL, :]
                    total = w[0] * here
                    sums[0] = sums[0] + here * xs[b, s, HALO + at_row : HALO + at_row + SUBL, :]
                    for o in range(1, tap_count):
                        total = total + w[o] * fg[s, at_row + o : at_row + o + SUBL, :]
                        sums[o] = sums[o] + here * xs[b, s, HALO + at_row - o : HALO + at_row - o + SUBL, :]
                    parts.append(total)
                ig[s, 16 * r : 16 * r + 16, lo] = jnp.concatenate(parts, axis=0).astype(ig.dtype)
            for o in range(tap_count):
                at_out = base + s * tap_count + o
                grads[b, at_out : at_out + 1, :] = jnp.sum(sums[o], axis=0, keepdims=True)

        @pl.when(b != me_g)
        def _():
            rs_copy(b).start()

        return carry

    lax.fori_loop(0, blocks, second, 0)

    others = [lax.rem(me_g + k, group) for k in range(1, group)]
    total = grads[me_g]
    for p in others:
        remote(grads.at[p], rs.at[p], rs_send.at[p], rs_recv.at[p], peer(p)).wait_recv()
        total = total + rs[p]
    ag[me_g] = total
    for p in others:
        remote(ag.at[me_g], ag.at[me_g], ag_send.at[p], ag_recv.at[me_g], peer(p)).start()
    square = total * total
    res_sq = jnp.sum(square[0:order, :], axis=0, keepdims=True)
    rate_sq = jnp.sum(square[order : 2 * order, :], axis=0, keepdims=True)
    skip_at = 2 * order + 3 * tap_count
    skip_sq = square[skip_at : skip_at + 1, :]
    rest_sq = jnp.sum(
        jnp.where(lax.broadcasted_iota(jnp.int32, (grad_rows - 2 * order, LANES), 0) < 3 * tap_count,
                  square[2 * order :, :], 0.0), axis=0, keepdims=True)
    rows_at = iota_rows()
    tile = jnp.where(rows_at == 0, res_sq, jnp.where(rows_at == 1, rate_sq,
                     jnp.where(rows_at == 2, rest_sq, jnp.where(rows_at == 3, skip_sq, 0.0))))
    tot[...] = tile
    tps = [lax.rem(me_tp + k, ntp) for k in range(1, ntp)]
    for q in tps:
        remote(tot, tot_tp.at[me_tp], tp_send.at[q], tp_recv.at[me_tp], {"tp": q}).start()
    for q in tps:
        remote(tot, tot_tp.at[q], tp_send.at[q], tp_recv.at[q], {"tp": q}).wait_recv()
        tile = tile + tot_tp[q]
    tot_all[me_g] = tile
    for p in others:
        remote(tot_all.at[me_g], tot_all.at[me_g], all_send.at[p], all_recv.at[me_g], peer(p)).start()
    for p in others:
        remote(tot_all.at[p], tot_all.at[p], all_send.at[p], all_recv.at[p], peer(p)).wait_recv()
        tile = tile + tot_all[p]
    sums = jnp.sum(tile, axis=1, keepdims=True)
    full = width * ntp
    counts = (order * full, order * full, 3 * tap_count * full, full)
    scales = [1.0 / jnp.maximum(1.0, jnp.sqrt(sums[k : k + 1, :] * (1.0 / counts[k]))) for k in range(4)]
    which = lax.broadcasted_iota(jnp.int32, (grad_rows, 1), 0)
    scale = jnp.where(which < order, scales[0], jnp.where(which < 2 * order, scales[1],
                      jnp.where(which < skip_at, scales[2], scales[3])))
    scale = jnp.broadcast_to(scale, (grad_rows, LANES))
    upd[:, lanes(me_g)] = ag[me_g] * scale
    for p in others:
        remote(ag.at[p], ag.at[p], ag_send.at[p], ag_recv.at[p], peer(p)).wait_recv()
        upd[:, lanes(p)] = ag[p] * scale

    @pl.when(me < nctx - 1)
    def _():
        down.wait_send()

    @pl.when(me > 0)
    def _():
        up.wait_send()
        upc.wait_send()

    def drain(b, carry):
        for far in range(1, nctx):
            @pl.when(me + far < nctx)
            def _():
                f_copy(b, far).wait_send()

            @pl.when(me >= far)
            def _():
                b_copy(b, far).wait_send()
        return carry

    lax.fori_loop(0, blocks, drain, 0)
    for p in others:
        rs_copy(p).wait_send()
        remote(ag.at[me_g], ag.at[me_g], ag_send.at[p], ag_recv.at[me_g], peer(p)).wait_send()
        remote(tot_all.at[me_g], tot_all.at[me_g], all_send.at[p], all_recv.at[me_g], peer(p)).wait_send()
    for q in tps:
        remote(tot, tot_tp.at[me_tp], tp_send.at[q], tp_recv.at[me_tp], {"tp": q}).wait_send()


def fused(projected, cotangent, conv_taps, residues, decay_rates, skip_gain):
    ndp, nctx, ntp = (lax.axis_size(a) for a in ("dp", "ctx", "tp"))
    _, _, tok, width = projected.shape
    order = residues.shape[0]
    tap_count = conv_taps.shape[1]
    blocks = width // LANES
    group = ndp * nctx
    seg = (tok + HALO) // SUBL
    grad_rows = -(-(2 * order + 3 * tap_count + 1) // SUBL) * SUBL
    vm = pl.BlockSpec(memory_space=pltpu.VMEM)
    dma = pltpu.SemaphoreType.DMA
    V = pltpu.VMEM
    bf = jnp.bfloat16
    mixed, ig, upd = pl.pallas_call(
        functools.partial(mega, (ndp, nctx, ntp, order, tap_count)),
        out_shape=(
            jax.ShapeDtypeStruct((tok, width), bf),
            jax.ShapeDtypeStruct((3, tok, width), bf),
            jax.ShapeDtypeStruct((grad_rows, width), F32),
        ),
        in_specs=[vm] * 7,
        out_specs=(vm, vm, vm),
        scratch_shapes=[
            V((3, HALO, width), bf), V((3, HALO, width), bf), V((HALO, width), bf),
            V((blocks, 3, tok + 2 * HALO, LANES), F32), V((blocks, tok + HALO, LANES), F32),
            V((blocks, 3, seg * SUBL, LANES), F32), V((blocks, seg * SUBL, LANES), F32),
            V((blocks, seg * SUBL, LANES), F32),
            V((blocks, order, SUBL, LANES), F32), V((blocks, order, SUBL, LANES), F32),
            V((blocks, order, LANES), F32), V((blocks, order, LANES), F32),
            V((nctx - 1, blocks, order, LANES), F32), V((nctx - 1, blocks, order, LANES), F32),
            V((8, blocks, order, LANES), F32), V((order, LANES), F32), V((order, LANES), F32),
            V((seg * SUBL, LANES), F32), V((seg * SUBL, LANES), F32),
            V((GROUP, seg, SUBL, LANES), F32), V((order, LANES), F32), V((order, LANES), F32),
            V((seg * SUBL, LANES), F32), V((3, seg * SUBL, LANES), F32),
            V((blocks, grad_rows, LANES), F32), V((group, grad_rows, LANES), F32),
            V((group, grad_rows, LANES), F32),
            V((SUBL, LANES), F32), V((ntp, SUBL, LANES), F32), V((group, SUBL, LANES), F32),
            dma((3,)), dma((3,)),
            dma((nctx - 1, blocks)), dma((nctx - 1, blocks)), dma((nctx - 1, blocks)), dma((nctx - 1, blocks)),
            dma((group,)), dma((group,)), dma((group,)), dma((group,)),
            dma((ntp,)), dma((ntp,)), dma((group,)), dma((group,)),
        ],
        compiler_params=pltpu.CompilerParams(
            collective_id=0, has_side_effects=True, vmem_limit_bytes=48 * 1024 * 1024),
    )(projected[0], cotangent[0], conv_taps.reshape(3 * tap_count, width), residues, decay_rates,
      skip_gain.reshape(1, width), jnp.sqrt(-jnp.expm1(-2.0 * decay_rates)))
    base = 2 * order
    return (mixed[None], ig[None],
            upd[base : base + 3 * tap_count].reshape(3, tap_count, width),
            upd[0:order], upd[order:base], upd[base + 3 * tap_count])


def fits(mesh, projected, residues, conv_taps):
    tok = projected.shape[2] // mesh.shape["ctx"]
    width = projected.shape[3] // mesh.shape["tp"]
    group = mesh.shape["dp"] * mesh.shape["ctx"]
    return (width == group * LANES and tok % 16 == 0 and tok >= 64 and mesh.shape["ctx"] > 1
            and mesh.shape["tp"] > 1 and residues.shape[0] % SUBL == 0
            and conv_taps.shape[1] <= HALO - 1 and projected.shape[0] == mesh.shape["dp"])


def solution(mesh):
    in_specs = (
        P("dp", None, "ctx", "tp"),
        P("dp", "ctx", "tp"),
        P(None, None, "tp"),
        P(None, "tp"),
        P(None, "tp"),
        P("tp"),
    )
    out_specs = (
        P("dp", "ctx", "tp"),
        P("dp", None, "ctx", "tp"),
        P(None, None, "tp"),
        P(None, "tp"),
        P(None, "tp"),
        P("tp"),
    )

    def run(projected, cotangent, conv_taps, residues, decay_rates, skip_gain):
        body = fused if fits(mesh, projected, residues, conv_taps) else local
        mapped = jax.shard_map(body, mesh=mesh, in_specs=in_specs, out_specs=out_specs, check_vma=False)
        return mapped(projected, cotangent, conv_taps, residues, decay_rates, skip_gain)

    return run
```

profile of v0, /device:TPU:0, one launch (start us, length us, event | category | flops | bytes accessed | tf_op | source)
XLA Modules:
  0.0 42.2 jit_solution(7816464506614547987)
XLA Ops:
  0.6 0.0 copy-start.1
  0.6 0.9 %negate_sqrt_fusion.norm = f32[16,1024]{1,0:T(8,128)S(1)} fusion(f32[16,1024]{1,0:T(8,128)} %rate.1), kind=kLoop, calls=%fused_computation | loop fusion | flops 32768 | bytes 131072 | tf_op jit(solution)/shard_map/sqrt | solution.py:570
  1.6 0.0 copy-start.2
  1.6 0.0 copy-start.4
  1.6 0.9 %reshape.21.taps = f32[21,1024]{1,0:T(8,128)S(1)} reshape(f32[3,7,1024]{2,1,0:T(8,128)} %param.8) | data formatting | bytes 172032 | tf_op jit(solution)/shard_map/reshape | solution.py:569
  2.5 0.0 copy-done.1
  2.5 0.0 copy-done.2
  2.6 0.0 copy-done.4
  2.6 0.0 copy-start
  2.6 1.1 %copy-done = bf16[1,3,128,1024]{3,2,1,0:T(8,128)(2,1)S(1)} copy-done((bf16[1,3,128,1024]{3,2,1,0:T(8,128)(2,1)S(1)}, bf16[1,3,128,1024]{3,2,1,0:T(8,128)(2,1)}, u32[]{:S(2)}) %copy-start) | copy-done | bytes 786456
  3.7 0.0 copy-start.3
  3.7 0.8 %copy-done.3 = f32[16,1024]{1,0:T(8,128)S(1)} copy-done((f32[16,1024]{1,0:T(8,128)S(1)}, f32[16,1024]{1,0:T(8,128)}, u32[]{:S(2)}) %copy-start.3) | copy-done | bytes 65560
  4.5 34.1 %shard_map.109 = (bf16[128,1024]{1,0:T(8,128)(2,1)S(1)}, bf16[3,128,1024]{2,1,0:T(8,128)(2,1)S(1)}, f32[56,1024]{1,0:T(8,128)S(1)}) custom-call(bf16[3,128,1024]{2,1,0:T(8,128)(2,1)S(1)} %bitcast.7, bf16[128,1024]{1,0:T(8,128)(2,1)S(1)} %bitcast.9, f32[21,1024]{1,0:T(8,128)S(1)} %reshape.21.taps, f32[16,1024]{1,0:T(8,128)S(1)} %copy-done.3, ...), custom_call_target="tpu_custom_call" | custom-call | tf_op jit(solution)/shard_map/pallas_call | solution.py:538
  38.7 0.6 %slice.15 = f32[1,1024]{1,0:T(1,128)} slice(f32[56,1024]{1,0:T(8,128)S(1)} %get-tuple-element.11), slice={[53:54], [0:1024]} | slice | bytes 8192 | tf_op jit(solution)/shard_map/slice | solution.py:574
  39.3 0.7 %fusion = (f32[16,1024]{1,0:T(8,128)}, f32[16,1024]{1,0:T(8,128)}) fusion(f32[56,1024]{1,0:T(8,128)S(1)} %get-tuple-element.11), kind=kLoop, calls=%fused_computation.1 | loop fusion | bytes 262144 | tf_op jit(solution)/shard_map/slice | solution.py:574
  39.9 0.7 %reshape.23 = f32[3,7,1024]{2,1,0:T(8,128)} reshape(f32[21,1024]{1,0:T(8,128)S(1)} %slice.12) | data formatting | bytes 172032 | tf_op jit(solution)/shard_map/reshape | solution.py:573
  40.6 0.7 %copy.14 = bf16[1,128,1024]{2,1,0:T(8,128)(2,1)} copy(bf16[1,128,1024]{2,1,0:T(8,128)(2,1)S(1)} %bitcast.8) | data formatting | bytes 524288
  41.3 0.9 %copy.15 = bf16[1,3,128,1024]{3,2,1,0:T(8,128)(2,1)} copy(bf16[1,3,128,1024]{3,2,1,0:T(8,128)(2,1)S(1)} %bitcast.6) | data formatting | bytes 1572864
  (1 shorter events, 0.0 us)
Async XLA Ops:
  0.6 1.9 %copy-start.1 = (bf16[1,128,1024]{2,1,0:T(8,128)(2,1)S(1)}, bf16[1,128,1024]{2,1,0:T(8,128)(2,1)}, u32[]{:S(2)}) copy-start(bf16[1,128,1024]{2,1,0:T(8,128)(2,1)} %param.7) | copy-start | bytes 786436
  1.6 1.0 %copy-start.2 = (f32[16,1024]{1,0:T(8,128)S(1)}, f32[16,1024]{1,0:T(8,128)}, u32[]{:S(2)}) copy-start(f32[16,1024]{1,0:T(8,128)} %rate.1) | copy-start | bytes 196612
  1.6 1.0 %copy-start.4 = (f32[1024]{0:T(1024)S(1)}, f32[1024]{0:T(1024)}, u32[]{:S(2)}) copy-start(f32[1024]{0:T(1024)} %param.11) | copy-start | bytes 12292
  2.6 1.1 %copy-start = (bf16[1,3,128,1024]{3,2,1,0:T(8,128)(2,1)S(1)}, bf16[1,3,128,1024]{3,2,1,0:T(8,128)(2,1)}, u32[]{:S(2)}) copy-start(bf16[1,3,128,1024]{3,2,1,0:T(8,128)(2,1)} %param.6) | copy-start | bytes 2359300
  3.7 0.8 %copy-start.3 = (f32[16,1024]{1,0:T(8,128)S(1)}, f32[16,1024]{1,0:T(8,128)}, u32[]{:S(2)}) copy-start(f32[16,1024]{1,0:T(8,128)} %res.1) | copy-start | bytes 196612
where the time goes:
time: 42.4 us; the launch traced here: 42.2 us
  Pallas kernels  34.1 us (80%)
  local copies, waits for them, and re-layouts  6.42 us (15%)
  other arithmetic  0.93 us (2%)
  between operations  0.7 us (2%)
    pallas_call x1, Pallas kernels, fused(): pl.pallas_call(functools.partial(mega, (ndp, nctx, ntp, order, tap_count)...  34.1 us
    unnamed x12, local copies, waits for them, and re-layouts  3.57 us
    reshape x1, local copies, waits for them, and re-layouts, fused(): conv_taps.reshape(3 * tap_count, width)  0.94 us
    sqrt x1, other arithmetic, fused(): jnp.sqrt(-jnp.expm1(-2.0 * decay_rates))  0.93 us

commit v1 on v0

--- a/solution.py
+++ b/solution.py
@@ -144,6 +144,7 @@
 SUBL = 8
 HALO = 8
 GROUP = 4
+GRANT = 62 * 1024 * 1024
 MESH = pl.DeviceIdType.MESH
 F32 = jnp.float32
 
@@ -152,8 +153,9 @@
     return lax.broadcasted_iota(jnp.int32, (SUBL, LANES), 0)
 
 
-def mega(sizes, x, cot, taps, res, rate, skip, norm, mixed, ig, upd,
-         prev, nxt, nct, xs, ct, feat, drive, gz, pre_f, pre_b, sum_f, sum_b, got_f, got_b,
+def mega(sizes, x_hbm, cot_hbm, taps_hbm, res_hbm, rate_hbm, skip_hbm,
+         mixed, ig, taps_upd, res_upd, rate_upd, skip_upd,
+         x, cot, taps, res, rate, skip, load_sem, prev, nxt, nct, xs, ct, feat, drive, gz, pre_f, pre_b, sum_f, sum_b, got_f, got_b,
          tab, in_f, in_b, lt, at, hist, acc_c, acc_d, ms, fg, grads, rs, ag, tot, tot_tp, tot_all,
          halo_send, halo_recv, f_send, f_recv, b_send, b_recv,
          rs_send, rs_recv, ag_send, ag_recv, tp_send, tp_recv, all_send, all_recv):
@@ -172,6 +174,10 @@
     def peer(p):
         return {"dp": p // nctx, "ctx": lax.rem(p, nctx)}
 
+    pairs = ((rate_hbm, rate), (x_hbm, x), (cot_hbm, cot), (res_hbm, res), (taps_hbm, taps), (skip_hbm, skip))
+    loads = [pltpu.make_async_copy(src, dst, load_sem.at[k]) for k, (src, dst) in enumerate(pairs)]
+    for load in loads:
+        load.start()
     barrier = pltpu.get_barrier_semaphore()
     for k in range(1, group):
         p = lax.rem(me_g + k, group)
@@ -179,47 +185,6 @@
     for k in range(1, ntp):
         q = lax.rem(me_tp + k, ntp)
         pl.semaphore_signal(barrier, inc=1, device_id={"tp": q}, device_id_type=MESH)
-    pl.semaphore_wait(barrier, group - 1 + ntp - 1)
-
-    def remote(src, dst, send, recv, where):
-        return pltpu.make_async_remote_copy(
-            src_ref=src, dst_ref=dst, send_sem=send, recv_sem=recv,
-            device_id=where, device_id_type=MESH)
-
-    down = remote(x.at[:, pl.ds(tok - HALO, HALO), :], prev, halo_send.at[0], halo_recv.at[0],
-                  {"ctx": jnp.minimum(me + 1, nctx - 1)})
-    up = remote(x.at[:, pl.ds(0, HALO), :], nxt, halo_send.at[1], halo_recv.at[1],
-                {"ctx": jnp.maximum(me - 1, 0)})
-    upc = remote(cot.at[pl.ds(0, HALO), :], nct, halo_send.at[2], halo_recv.at[2],
-                 {"ctx": jnp.maximum(me - 1, 0)})
-
-    @pl.when(me < nctx - 1)
-    def _():
-        down.start()
-
-    @pl.when(me > 0)
-    def _():
-        up.start()
-        upc.start()
-
-    @pl.when(me == 0)
-    def _():
-        prev[...] = jnp.zeros_like(prev)
-
-    @pl.when(me == nctx - 1)
-    def _():
-        nxt[...] = jnp.zeros_like(nxt)
-        nct[...] = jnp.zeros_like(nct)
-
-    @pl.when(me > 0)
-    def _():
-        down.wait_recv()
-
-    @pl.when(me < nctx - 1)
-    def _():
-        up.wait_recv()
-        upc.wait_recv()
-
     def lanes(b):
         return pl.ds(pl.multiple_of(b * LANES, LANES), LANES)
 
@@ -235,16 +200,13 @@
     def strided(j):
         return pl.ds(j, SUBL, stride=seg)
 
-    def f_copy(b, far):
-        return remote(sum_f.at[b], got_f.at[far - 1, b], f_send.at[far - 1, b], f_recv.at[far - 1, b],
-                      {"ctx": jnp.minimum(me + far, nctx - 1)})
-
-    def b_copy(b, far):
-        return remote(sum_b.at[b], got_b.at[far - 1, b], b_send.at[far - 1, b], b_recv.at[far - 1, b],
-                      {"ctx": jnp.maximum(me - far, 0)})
-
-    def first(i, carry):
-        b = lax.rem(me_g + 1 + i, blocks)
+    def turn(i):
+        return lax.rem(i + me_dp * (blocks // ndp), blocks)
+
+    for load in loads:
+        load.wait()
+
+    def fill(b, carry):
         lo = lanes(b)
         rates = rate[:, lo]
         tab[0, b] = jnp.exp(-rates)
@@ -252,20 +214,82 @@
         tab[2, b] = jnp.exp(-rates * (2 * seg))
         tab[3, b] = jnp.exp(-rates * (4 * seg))
         tab[4, b] = jnp.exp(-rates * (seg - HALO))
-        root = norm[:, lo]
+        twice = 2.0 * rates
+        series = jnp.ones_like(twice)
+        for k in range(12, 1, -1):
+            series = 1.0 - twice * series * (1.0 / k)
+        root = jnp.sqrt(jnp.where(twice < 0.5, twice * series, 1.0 - jnp.exp(-twice)))
         tab[5, b] = root
         tab[6, b] = res[:, lo] * root
         tab[7, b] = rates
         for s in range(3):
+            for r in range(tok // 16):
+                xs[b, s, HALO + 16 * r : HALO + 16 * r + 16, :] = x[s, 16 * r : 16 * r + 16, lo].astype(F32)
+        for r in range(tok // 16):
+            ct[b, 16 * r : 16 * r + 16, :] = cot[16 * r : 16 * r + 16, lo].astype(F32)
+        return carry
+
+    lax.fori_loop(0, blocks // 2, fill, 0)
+    pl.semaphore_wait(barrier, group - 1 + ntp - 1)
+
+    def remote(src, dst, send, recv, where):
+        return pltpu.make_async_remote_copy(
+            src_ref=src, dst_ref=dst, send_sem=send, recv_sem=recv,
+            device_id=where, device_id_type=MESH)
+
+    down = remote(x_hbm.at[:, pl.ds(tok - HALO, HALO), :], prev, halo_send.at[0], halo_recv.at[0],
+                  {"ctx": jnp.minimum(me + 1, nctx - 1)})
+    up = remote(x_hbm.at[:, pl.ds(0, HALO), :], nxt, halo_send.at[1], halo_recv.at[1],
+                {"ctx": jnp.maximum(me - 1, 0)})
+    upc = remote(cot_hbm.at[pl.ds(0, HALO), :], nct, halo_send.at[2], halo_recv.at[2],
+                 {"ctx": jnp.maximum(me - 1, 0)})
+
+    @pl.when(me < nctx - 1)
+    def _():
+        down.start()
+
+    @pl.when(me > 0)
+    def _():
+        up.start()
+        upc.start()
+
+    @pl.when(me == 0)
+    def _():
+        prev[...] = jnp.zeros_like(prev)
+
+    @pl.when(me == nctx - 1)
+    def _():
+        nxt[...] = jnp.zeros_like(nxt)
+        nct[...] = jnp.zeros_like(nct)
+
+    lax.fori_loop(blocks // 2, blocks, fill, 0)
+
+    @pl.when(me > 0)
+    def _():
+        down.wait_recv()
+
+    @pl.when(me < nctx - 1)
+    def _():
+        up.wait_recv()
+        upc.wait_recv()
+
+    def f_copy(b, far):
+        return remote(sum_f.at[b], got_f.at[far - 1, b], f_send.at[far - 1, b], f_recv.at[far - 1, b],
+                      {"ctx": jnp.minimum(me + far, nctx - 1)})
+
+    def b_copy(b, far):
+        return remote(sum_b.at[b], got_b.at[far - 1, b], b_send.at[far - 1, b], b_recv.at[far - 1, b],
+                      {"ctx": jnp.maximum(me - far, 0)})
+
+    def first(i, carry):
+        b = turn(i)
+        lo = lanes(b)
+        for s in range(3):
             xs[b, s, 0:HALO, :] = prev[s, :, lo].astype(F32)
             xs[b, s, tok + HALO : tok + 2 * HALO, :] = nxt[s, :, lo].astype(F32)
-            for r in range(tok // 16):
-                xs[b, s, HALO + 16 * r : HALO + 16 * r + 16, :] = x[s, 16 * r : 16 * r + 16, lo].astype(F32)
         ct[b, tok : tok + HALO, :] = nct[:, lo].astype(F32)
-        for r in range(tok // 16):
-            ct[b, 16 * r : 16 * r + 16, :] = cot[16 * r : 16 * r + 16, lo].astype(F32)
         for s in range(3):
-            w = [row(taps, s * tap_count + o, b) for o in range(tap_count)]
+            w = [jnp.broadcast_to(taps[s, o : o + 1, lo], (SUBL, LANES)) for o in range(tap_count)]
             for j in range(seg):
                 total = w[0] * xs[b, s, strided(HALO + j), :]
                 for o in range(1, tap_count):
@@ -325,7 +349,7 @@
         return remote(grads.at[b], rs.at[me_g], rs_send.at[b], rs_recv.at[me_g], peer(b))
 
     def second(i, carry):
-        b = lax.rem(me_g + 1 + i, blocks)
+        b = turn(i)
         lo = lanes(b)
         rates = rate[:, lo]
         in_f[...] = jnp.zeros_like(in_f)
@@ -422,7 +446,7 @@
         for r in range(tok // 16):
             mixed[16 * r : 16 * r + 16, lo] = ms[16 * r : 16 * r + 16, :].astype(mixed.dtype)
         for s in range(3):
-            w = [row(taps, s * tap_count + o, b) for o in range(tap_count)]
+            w = [jnp.broadcast_to(taps[s, o : o + 1, lo], (SUBL, LANES)) for o in range(tap_count)]
             sums = [zero] * tap_count
             for r in range(tok // 16):
                 parts = []
@@ -488,10 +512,20 @@
     scale = jnp.where(which < order, scales[0], jnp.where(which < 2 * order, scales[1],
                       jnp.where(which < skip_at, scales[2], scales[3])))
     scale = jnp.broadcast_to(scale, (grad_rows, LANES))
-    upd[:, lanes(me_g)] = ag[me_g] * scale
+    def write(p):
+        lo = lanes(p)
+        block = ag[p] * scale
+        res_upd[:, lo] = block[0:order, :]
+        rate_upd[:, lo] = block[order : 2 * order, :]
+        for s in range(3):
+            at_row = 2 * order + s * tap_count
+            taps_upd[s, :, lo] = block[at_row : at_row + tap_count, :]
+        skip_upd[:, lo] = block[skip_at : skip_at + 1, :]
+
+    write(me_g)
     for p in others:
         remote(ag.at[p], ag.at[p], ag_send.at[p], ag_recv.at[p], peer(p)).wait_recv()
-        upd[:, lanes(p)] = ag[p] * scale
+        write(p)
 
     @pl.when(me < nctx - 1)
     def _():
@@ -520,6 +554,15 @@
         remote(tot_all.at[me_g], tot_all.at[me_g], all_send.at[p], all_recv.at[me_g], peer(p)).wait_send()
     for q in tps:
         remote(tot, tot_tp.at[me_tp], tp_send.at[q], tp_recv.at[me_tp], {"tp": q}).wait_send()
+
+
+def place(*refs):
+    sem = refs[-1]
+    copies = [pltpu.make_async_copy(refs[k], refs[6 + k], sem.at[k]) for k in range(6)]
+    for copy in copies:
+        copy.start()
+    for copy in copies:
+        copy.wait()
 
 
 def fused(projected, cotangent, conv_taps, residues, decay_rates, skip_gain):
@@ -535,16 +578,23 @@
     dma = pltpu.SemaphoreType.DMA
     V = pltpu.VMEM
     bf = jnp.bfloat16
-    mixed, ig, upd = pl.pallas_call(
+    shapes = (
+        jax.ShapeDtypeStruct((tok, width), bf),
+        jax.ShapeDtypeStruct((3, tok, width), bf),
+        jax.ShapeDtypeStruct((3, tap_count, width), F32),
+        jax.ShapeDtypeStruct((order, width), F32),
+        jax.ShapeDtypeStruct((order, width), F32),
+        jax.ShapeDtypeStruct((1, width), F32),
+    )
+    hbm = pl.BlockSpec(memory_space=pltpu.HBM)
+    parts = pl.pallas_call(
         functools.partial(mega, (ndp, nctx, ntp, order, tap_count)),
-        out_shape=(
-            jax.ShapeDtypeStruct((tok, width), bf),
-            jax.ShapeDtypeStruct((3, tok, width), bf),
-            jax.ShapeDtypeStruct((grad_rows, width), F32),
-        ),
-        in_specs=[vm] * 7,
-        out_specs=(vm, vm, vm),
+        out_shape=shapes,
+        in_specs=[hbm] * 6,
+        out_specs=(vm,) * 6,
         scratch_shapes=[
+            V((3, tok, width), bf), V((tok, width), bf), V((3, tap_count, width), F32),
+            V((order, width), F32), V((order, width), F32), V((1, width), F32), dma((6,)),
             V((3, HALO, width), bf), V((3, HALO, width), bf), V((HALO, width), bf),
             V((blocks, 3, tok + 2 * HALO, LANES), F32), V((blocks, tok + HALO, LANES), F32),
             V((blocks, 3, seg * SUBL, LANES), F32), V((blocks, seg * SUBL, LANES), F32),
@@ -565,13 +615,16 @@
             dma((ntp,)), dma((ntp,)), dma((group,)), dma((group,)),
         ],
         compiler_params=pltpu.CompilerParams(
-            collective_id=0, has_side_effects=True, vmem_limit_bytes=48 * 1024 * 1024),
-    )(projected[0], cotangent[0], conv_taps.reshape(3 * tap_count, width), residues, decay_rates,
-      skip_gain.reshape(1, width), jnp.sqrt(-jnp.expm1(-2.0 * decay_rates)))
-    base = 2 * order
-    return (mixed[None], ig[None],
-            upd[base : base + 3 * tap_count].reshape(3, tap_count, width),
-            upd[0:order], upd[order:base], upd[base + 3 * tap_count])
+            collective_id=0, has_side_effects=True, vmem_limit_bytes=GRANT),
+    )(projected[0], cotangent[0], conv_taps, residues, decay_rates, skip_gain.reshape(1, width))
+    mixed, ig, taps_upd, res_upd, rate_upd, skip_upd = pl.pallas_call(
+        place,
+        out_shape=shapes,
+        in_specs=[vm] * 6,
+        out_specs=(hbm,) * 6,
+        scratch_shapes=[dma((6,))],
+    )(*parts)
+    return mixed[None], ig[None], taps_upd, res_upd, rate_upd, skip_upd.reshape(width)
 
 
 def fits(mesh, projected, residues, conv_taps):

time: 42.4 us -> 36.8 us (0.87)
  local copies, waits for them, and re-layouts: 6.42 us -> 0 us
  Pallas kernels: 34.1 us -> 36 us
  other arithmetic: 0.93 us -> 0 us
    unnamed x12 -> x0, local copies, waits for them, and re-layouts: 3.57 us -> none
    pallas_call x0 -> x1, Pallas kernels: none -> 2.32 us  [fused(): pl.pallas_call(place, out_shape=shapes, in_specs=[vm] * 6, out_specs=(hbm...]
    reshape x2 -> x0, local copies, waits for them, and re-layouts: 1.59 us -> none  [the longest x1 0.94 us: fused(): conv_taps.reshape(3 * tap_count, width)]
    slice x3 -> x0, local copies, waits for them, and re-layouts: 1.26 us -> none  [the longest x1 0.66 us: fused(): upd[order:base]]
    sqrt x1 -> x0, other arithmetic: 0.93 us -> none  [fused(): jnp.sqrt(-jnp.expm1(-2.0 * decay_rates))]
where the time goes in v1:
time: 36.8 us; the launch traced here: 36.7 us
  Pallas kernels  36 us (98%)
  between operations  0.64 us (2%)
    pallas_call x1, Pallas kernels, fused(): pl.pallas_call(functools.partial(mega, (ndp, nctx, ntp, order, tap_count)...  33.7 us
    pallas_call x1, Pallas kernels, fused(): pl.pallas_call(place, out_shape=shapes, in_specs=[vm] * 6, out_specs=(hbm...  2.32 us

profile of v1, /device:TPU:0, one launch (start us, length us, event | category | flops | bytes accessed | tf_op | source)
XLA Modules:
  0.0 36.7 jit_solution(6999620647285678574)
XLA Ops:
  0.6 33.7 %shard_map.109 = (bf16[128,1024]{1,0:T(8,128)(2,1)}, bf16[3,128,1024]{2,1,0:T(8,128)(2,1)}, f32[3,7,1024]{2,1,0:T(8,128)}, f32[16,1024]{1,0:T(8,128)}, f32[16,1024]{1,0:T(8,128)}, /*index=5*/f32[1,1024]{1,0:T(1,128)}) custom-call(bf16[3,128,1024]{2,1,0:T(8,128)(2,1)} %bitcast.6, bf16[128,1024]{1,0:T(8,128)(2,1)} %bitcast.7, f32[3,7,1024]{2,1,0:T(8,128)} %taps_hbm.1, ...), custom_call_target="tpu_custom_call" | custom-call | tf_op jit(solution)/shard_map/pallas_call | solution.py:590
  34.4 2.3 %shard_map.110 = (bf16[128,1024]{1,0:T(8,128)(2,1)}, bf16[3,128,1024]{2,1,0:T(8,128)(2,1)}, f32[3,7,1024]{2,1,0:T(8,128)}, f32[16,1024]{1,0:T(8,128)}, f32[16,1024]{1,0:T(8,128)}, /*index=5*/f32[1,1024]{1,0:T(1,128)}) custom-call(bf16[128,1024]{1,0:T(8,128)(2,1)} %get-tuple-element.18.refs_0_, bf16[3,128,1024]{2,1,0:T(8,128)(2,1)} %get-tuple-element.19.refs_1_, ...), custom_call_target="tpu_custom_call" | custom-call | tf_op jit(solution)/shard_map/pallas_call | solution.py:620

commit v2 on v1

--- a/solution.py
+++ b/solution.py
@@ -154,8 +154,8 @@
 
 
 def mega(sizes, x_hbm, cot_hbm, taps_hbm, res_hbm, rate_hbm, skip_hbm,
-         mixed, ig, taps_upd, res_upd, rate_upd, skip_upd,
-         x, cot, taps, res, rate, skip, load_sem, prev, nxt, nct, xs, ct, feat, drive, gz, pre_f, pre_b, sum_f, sum_b, got_f, got_b,
+         mixed_hbm, ig_hbm, taps_upd, res_upd, rate_upd, skip_upd,
+         x, cot, taps, res, rate, skip, load_sem, mixed, ig, out_sem, prev, nxt, nct, xs, ct, feat, drive, gz, pre_f, pre_b, sum_f, sum_b, got_f, got_b,
          tab, in_f, in_b, lt, at, hist, acc_c, acc_d, ms, fg, grads, rs, ag, tot, tot_tp, tot_all,
          halo_send, halo_recv, f_send, f_recv, b_send, b_recv,
          rs_send, rs_recv, ag_send, ag_recv, tp_send, tp_recv, all_send, all_recv):
@@ -347,6 +347,11 @@
 
     def rs_copy(b):
         return remote(grads.at[b], rs.at[me_g], rs_send.at[b], rs_recv.at[me_g], peer(b))
+
+    def out_copies(b):
+        lo = lanes(b)
+        return (pltpu.make_async_copy(mixed.at[:, lo], mixed_hbm.at[:, lo], out_sem.at[0, b]),
+                pltpu.make_async_copy(ig.at[:, :, lo], ig_hbm.at[:, :, lo], out_sem.at[1, b]))
 
     def second(i, carry):
         b = turn(i)
@@ -468,6 +473,8 @@
         def _():
             rs_copy(b).start()
 
+        for copy in out_copies(b):
+            copy.start()
         return carry
 
     lax.fori_loop(0, blocks, second, 0)
@@ -537,6 +544,8 @@
         upc.wait_send()
 
     def drain(b, carry):
+        for copy in out_copies(b):
+            copy.wait()
         for far in range(1, nctx):
             @pl.when(me + far < nctx)
             def _():
@@ -591,10 +600,11 @@
         functools.partial(mega, (ndp, nctx, ntp, order, tap_count)),
         out_shape=shapes,
         in_specs=[hbm] * 6,
-        out_specs=(vm,) * 6,
+        out_specs=(hbm, hbm, vm, vm, vm, vm),
         scratch_shapes=[
             V((3, tok, width), bf), V((tok, width), bf), V((3, tap_count, width), F32),
             V((order, width), F32), V((order, width), F32), V((1, width), F32), dma((6,)),
+            V((tok, width), bf), V((3, tok, width), bf), dma((2, blocks)),
             V((3, HALO, width), bf), V((3, HALO, width), bf), V((HALO, width), bf),
             V((blocks, 3, tok + 2 * HALO, LANES), F32), V((blocks, tok + HALO, LANES), F32),
             V((blocks, 3, seg * SUBL, LANES), F32), V((blocks, seg * SUBL, LANES), F32),

time: 36.8 us -> 36.7 us (level)
  no operation moved by 1% of the time
where the time goes in v2:
time: 36.7 us; the launch traced here: 36.5 us
  Pallas kernels  35.8 us (98%)
  between operations  0.64 us (2%)
    pallas_call x1, Pallas kernels, fused(): pl.pallas_call(functools.partial(mega, (ndp, nctx, ntp, order, tap_count)...  33.5 us
    pallas_call x1, Pallas kernels, fused(): pl.pallas_call(place, out_shape=shapes, in_specs=[vm] * 6, out_specs=(hbm...  2.32 us

profile of v2, /device:TPU:0, one launch (start us, length us, event | category | flops | bytes accessed | tf_op | source)
XLA Modules:
  0.0 36.5 jit_solution(6145980951827034057)
XLA Ops:
  0.6 33.5 %shard_map.109 = (bf16[128,1024]{1,0:T(8,128)(2,1)}, bf16[3,128,1024]{2,1,0:T(8,128)(2,1)}, f32[3,7,1024]{2,1,0:T(8,128)}, f32[16,1024]{1,0:T(8,128)}, f32[16,1024]{1,0:T(8,128)}, /*index=5*/f32[1,1024]{1,0:T(1,128)}) custom-call(bf16[3,128,1024]{2,1,0:T(8,128)(2,1)} %bitcast.6, bf16[128,1024]{1,0:T(8,128)(2,1)} %bitcast.7, f32[3,7,1024]{2,1,0:T(8,128)} %taps_hbm.1, ...), custom_call_target="tpu_custom_call" | custom-call | tf_op jit(solution)/shard_map/pallas_call | solution.py:599
  34.2 2.3 %shard_map.110 = (bf16[128,1024]{1,0:T(8,128)(2,1)}, bf16[3,128,1024]{2,1,0:T(8,128)(2,1)}, f32[3,7,1024]{2,1,0:T(8,128)}, f32[16,1024]{1,0:T(8,128)}, f32[16,1024]{1,0:T(8,128)}, /*index=5*/f32[1,1024]{1,0:T(1,128)}) custom-call(bf16[128,1024]{1,0:T(8,128)(2,1)} %get-tuple-element.18.refs_0_, bf16[3,128,1024]{2,1,0:T(8,128)(2,1)} %get-tuple-element.19.refs_1_, ...), custom_call_target="tpu_custom_call" | custom-call | tf_op jit(solution)/shard_map/pallas_call | solution.py:630
